TPU v7x, 256 devices: a whole 4x4x8 slice. The times are simulated.
256 devices in a mesh: dp: 16 (over z, core), mp: 16 (over y, x).
Axes of the slice: x: 4, y: 4, z: 8, core: 2. Of those that a mesh axis runs over, the one named last changes fastest.
Arguments:
- candidates: bfloat16 [4096, 4096], P('dp', 'mp'), may hold values from -6 to 6
- hold_gate: bfloat16 [4096, 8192], P(None, 'mp'), may hold values from -0.09375 to 0.09375
- hold_up: bfloat16 [4096, 8192], P(None, 'mp'), may hold values from -0.09375 to 0.09375
- probe: float32 [8192], P('mp'), as said below
- chosen: int32 [16, 192], replicated, may hold values from 0 to 4095, as said below
- counts: int32 [16], replicated, may hold values from 24 to 192, as said below
- gate_w: bfloat16 [4096, 14336], P('dp', 'mp'), may hold values from -0.09375 to 0.09375
- up_w: bfloat16 [4096, 14336], P('dp', 'mp'), may hold values from -0.09375 to 0.09375
- cotangent: bfloat16 [3072, 14336], P('dp', 'mp'), may hold values from -6 to 6
Outputs:
- grad_gate: bfloat16 [4096, 14336], P('dp', 'mp')
- grad_up: bfloat16 [4096, 14336], P('dp', 'mp')
- hidden: bfloat16 [3072, 14336], P('dp', 'mp')
- cand_weight: float32 [4096], P('dp')
Inputs may be any that keep to these rules, and one draw needn't show every extreme that they name: `chosen`: all entries are distinct candidate indices. `counts`: exactly one training shard uses all 192 slots in every draw. `probe`: magnitudes at most 12 / sqrt(8192).
All inputs are finite; a program needn't handle non-finite values.
Results may differ from a plain program's by a relative error of at most 0.0057.
Values may be sent and summed in bfloat16 or wider, within the bound.
A program may use at most 128 MiB of HBM per device.

v0:
```python
import jax
import jax.numpy as jnp
from jax import lax
from jax.sharding import PartitionSpec as P


def gather_by_a2a(x, axis_name, axis):
    parts = lax.psum(1, axis_name)
    stacked = lax.all_to_all(
        jnp.broadcast_to(x[None], (parts,) + x.shape),
        axis_name,
        split_axis=0,
        concat_axis=0,
        tiled=True,
    )
    stacked = jnp.moveaxis(stacked, 0, axis)
    shape = list(x.shape)
    shape[axis] *= parts
    return stacked.reshape(shape)


def on_device(candidates, hold_gate, hold_up, probe, chosen, counts, gate_w, up_w, cotangent):
    cand_dev = candidates.shape[0]
    shards = chosen.shape[0]
    slots = chosen.shape[1]
    width = candidates.shape[1]
    ff = gate_w.shape[1]
    merged = lax.all_gather(jnp.concatenate([candidates, gate_w], axis=1), "dp", axis=0, tiled=True)
    all_cands = merged[:, :width]
    full_w = (merged[:, width:], lax.all_gather(up_w, "dp", axis=0, tiled=True))
    own_index = lax.axis_index("dp")
    source = chosen // cand_dev
    local_row = (chosen % cand_dev).reshape(-1)
    valid = jnp.arange(slots, dtype=jnp.int32)[None, :] < counts[:, None]
    usable = (valid & (source == own_index)).reshape(-1)
    onehot = (
        (local_row[:, None] == jnp.arange(cand_dev, dtype=jnp.int32)[None, :]) & usable[:, None]
    ).astype(jnp.bfloat16)
    own_chosen = lax.dynamic_index_in_dim(chosen, own_index, 0, keepdims=False)
    own_valid = lax.dynamic_index_in_dim(valid, own_index, 0, keepdims=False)
    own_onehot = (
        (own_chosen[:, None] == jnp.arange(all_cands.shape[0], dtype=jnp.int32)[None, :])
        & own_valid[:, None]
    ).astype(jnp.bfloat16)
    row_slab = jnp.dot(own_onehot, all_cands, preferred_element_type=jnp.float32).astype(
        jnp.bfloat16
    )
    row_x = gather_by_a2a(row_slab, "mp", 1)
    parts = lax.psum(1, "dp")
    row_blocks = row_x.reshape(row_x.shape[0], parts, -1).transpose(1, 0, 2)
    row_slices = lax.all_to_all(row_blocks, "dp", split_axis=0, concat_axis=0, tiled=True)
    row_slices = row_slices.reshape(-1, row_blocks.shape[2])
    incoming = gather_by_a2a(candidates, "mp", 1)
    hold_g = jnp.dot(incoming, hold_gate, preferred_element_type=jnp.float32)
    hold_u = jnp.dot(incoming, hold_up, preferred_element_type=jnp.float32)
    partial_score = jnp.sum(jax.nn.silu(hold_g) * hold_u * probe[None, :], axis=1)
    score = jnp.sum(gather_by_a2a(partial_score[None, :], "mp", 0), axis=0)
    cand_weight = jax.nn.sigmoid(score)
    picked_weight = (
        jnp.dot(
            onehot, cand_weight.astype(jnp.bfloat16)[:, None], preferred_element_type=jnp.float32
        )
        .astype(jnp.bfloat16)
        .reshape(shards, slots)
    )
    arrived_weight = lax.all_to_all(picked_weight, "dp", split_axis=0, concat_axis=0, tiled=True)
    row_weight = jnp.sum(arrived_weight.astype(jnp.float32), axis=0)
    gate = jnp.dot(row_x, full_w[0], preferred_element_type=jnp.float32)
    up = jnp.dot(row_x, full_w[1], preferred_element_type=jnp.float32)
    hidden = (jax.nn.silu(gate) * up).astype(jnp.bfloat16)
    back = cotangent.astype(jnp.float32) * row_weight[:, None]
    sig = jax.nn.sigmoid(gate)
    d_up = (back * gate * sig).astype(jnp.bfloat16)
    d_gate = (back * up * sig * (1.0 + gate * (1.0 - sig))).astype(jnp.bfloat16)
    contract_rows = (((0,), (0,)), ((), ()))
    d_both, row_slices = lax.optimization_barrier(
        (jnp.concatenate([d_gate, d_up], axis=1), row_slices)
    )
    both_d = lax.all_gather(d_both, "dp", axis=0, tiled=True)
    grads = lax.dot_general(
        row_slices, both_d, contract_rows, preferred_element_type=jnp.float32
    ).astype(jnp.bfloat16)
    return (grads[:, :ff], grads[:, ff:], hidden, cand_weight)


def solution(mesh):
    placed = (
        P("dp", "mp"),
        P(None, "mp"),
        P(None, "mp"),
        P("mp"),
        P(),
        P(),
        P("dp", "mp"),
        P("dp", "mp"),
        P("dp", "mp"),
    )
    return jax.shard_map(
        on_device,
        mesh=mesh,
        in_specs=placed,
        out_specs=(P("dp", "mp"), P("dp", "mp"), P("dp", "mp"), P("dp")),
        check_vma=False,
    )
```

profile of v0, /device:TPU:1, one launch (start us, length us, event | category | flops | bytes accessed | tf_op | source)
XLA Modules:
  0.0 239.8 jit_solution(12118811220462123746)
XLA Ops:
  7.2 0.0 copy-start
  7.2 0.0 all-gather.4.cloned.1.call-start
  7.2 1.9 pad_maximum_fusion.1
  9.2 0.0 all-gather.4.cloned.1.call-update
  9.2 0.0 all-gather.6.cloned.1.call-start
  9.2 0.7 all-gather.6.cloned.1.call-update
  9.9 0.0 copy-done
  10.0 0.1 copy.22
  10.1 1.5 broadcast_in_dim.6
  11.6 0.0 copy-start.1
  11.6 0.0 copy-start.2
  11.6 7.7 %all-to-all-start = ((bf16[16,256,256]{1,2,0:T(8,128)(2,1)}), bf16[16,256,256]{1,2,0:T(8,128)(2,1)S(1)}, u32[]{:S(2)}, u32[]{:S(2)}) async-start(bf16[16,256,256]{1,2,0:T(8,128)(2,1)} %broadcast_in_dim.6), calls=%async_computation | async-start | bytes 4194304 | tf_op jit(solution)/shard_map/all_to_all | solution.py:9
  19.3 0.0 copy-done.1
  19.3 0.0 copy-done.2
  19.3 0.1 fusion.22
  19.4 30.8 %all-to-all-done = bf16[16,256,256]{1,2,0:T(8,128)(2,1)S(1)} async-done(((bf16[16,256,256]{1,2,0:T(8,128)(2,1)}), bf16[16,256,256]{1,2,0:T(8,128)(2,1)S(1)}, u32[]{:S(2)}, u32[]{:S(2)}) %all-to-all-start) | async-done | bytes 2097184 | tf_op jit(solution)/shard_map/all_to_all | solution.py:9
  50.3 3.7 %fusion.26 = f32[256,512]{1,0:T(8,128)S(1)} fusion(bf16[256,4096]{0,1:T(8,128)(2,1)S(1)} %bitcast.20, bf16[4096,512]{1,0:T(8,128)(2,1)} %param.10), kind=kOutput, calls=%fused_computation.42 | convolution fusion | flops 1073741824 | bytes 6815744 | tf_op jit(solution)/shard_map/dot_general | solution.py:54
  54.0 0.0 copy-done.3
  54.0 0.0 copy-done.5
  54.0 1.4 fusion.14
  55.4 0.6 broadcast_in_dim.7
  56.0 3.9 %all-to-all-start.1 = ((f32[16,1,256]{2,1,0:T(1,128)}), f32[16,1,256]{2,1,0:T(1,128)S(1)}, u32[]{:S(2)}, u32[]{:S(2)}) async-start(f32[16,1,256]{2,1,0:T(1,128)} %broadcast_in_dim.7), calls=%async_computation.1 | async-start | bytes 32768 | tf_op jit(solution)/shard_map/all_to_all | solution.py:9
  59.9 0.1 and.37
  60.0 0.1 eq.38
  60.1 6.2 %all-to-all-done.1 = f32[16,1,256]{2,1,0:T(1,128)S(1)} async-done(((f32[16,1,256]{2,1,0:T(1,128)}), f32[16,1,256]{2,1,0:T(1,128)S(1)}, u32[]{:S(2)}, u32[]{:S(2)}) %all-to-all-start.1) | async-done | bytes 16416 | tf_op jit(solution)/shard_map/all_to_all | solution.py:9
  66.3 0.6 fusion.24
  66.9 2.5 %fusion.6 = f32[1,3072]{1,0:T(1,128)S(1)} fusion(bf16[256,1]{0,1:T(2,128)(2,1)S(1)} %reshape.45, s32[3072]{0:T(1024)S(1)} %eq.38, pred[3072]{0:T(1024)(128)(4,1)S(1)} %and.37), kind=kOutput, calls=%fused_computation.7 | convolution fusion | flops 3145728 | bytes 28160 | tf_op jit(solution)/shard_map/dot_general | solution.py:60
  69.4 0.7 all_to_all.24
  70.1 11.0 %all-to-all-start.2 = ((bf16[16,1,192]{2,1,0:T(2,128)(2,1)}), bf16[16,1,192]{2,1,0:T(2,128)(2,1)S(1)}, u32[]{:S(2)}, u32[]{:S(2)}) async-start(bf16[16,1,192]{2,1,0:T(2,128)(2,1)} %all_to_all.24), calls=%async_computation.2 | async-start | bytes 32768 | tf_op jit(solution)/shard_map/all_to_all | solution.py:66
  81.1 0.0 all-gather.4.cloned.1.call-done
  81.2 2.4 fusion.15
  83.5 4.9 %all-to-all-done.2 = bf16[16,1,192]{2,1,0:T(2,128)(2,1)S(1)} async-done(((bf16[16,1,192]{2,1,0:T(2,128)(2,1)}), bf16[16,1,192]{2,1,0:T(2,128)(2,1)S(1)}, u32[]{:S(2)}, u32[]{:S(2)}) %all-to-all-start.2) | async-done | bytes 6176 | tf_op jit(solution)/shard_map/all_to_all | solution.py:66
  88.5 0.1 broadcast_in_dim.8
  88.6 25.6 %all_to_all.30 = bf16[16,192,256]{2,1,0:T(8,128)(2,1)} all-to-all(bf16[16,192,256]{2,1,0:T(8,128)(2,1)S(1)} %broadcast_in_dim.8), channel_id=1, replica_groups=mesh['dp'=16,'mp'=16] {'mp'}, dimensions={0} | all-to-all | bytes 3145728 | tf_op jit(solution)/shard_map/all_to_all | solution.py:9
  114.2 5.0 %all-to-all-start.4 = ((bf16[16,192,256]{2,1,0:T(8,128)(2,1)}), bf16[16,192,256]{2,1,0:T(8,128)(2,1)S(1)}, u32[]{:S(2)}, u32[]{:S(2)}) async-start(bf16[16,192,256]{2,1,0:T(8,128)(2,1)} %all_to_all.30), calls=%async_computation.4 | async-start | bytes 3145728 | tf_op jit(solution)/shard_map/all_to_all | solution.py:51
  119.3 0.0 all-gather.8.cloned.1.call-start
  119.3 1.6 copy.27
  121.0 0.0 copy-start.4
  121.0 5.9 %fusion = f32[192,896]{1,0:T(8,128)} fusion(bf16[192,4096]{1,0:T(8,128)(2,1)S(1)} %bitcast.22, bf16[4096,1152]{1,0:T(8,128)(2,1)} %all-gather.4.cloned.1.call-done), kind=kOutput, calls=%fused_computation | convolution fusion | flops 1409286144 | bytes 9601024 | tf_op jit(solution)/shard_map/dot_general | solution.py:68
  126.9 1.1 all-gather.6.cloned.1.call-done
  128.0 0.0 copy-done.4
  128.0 5.9 %multiply_convert_fusion = (bf16[192,896]{1,0:T(8,128)(2,1)}, bf16[192,896]{1,0:T(8,128)(2,1)S(1)}, bf16[192,896]{1,0:T(8,128)(2,1)S(1)}) fusion(f32[192,896]{1,0:T(8,128)} %fusion, f32[192]{0:T(256)S(1)} %convert_reduce_fusion, bf16[192,896]{1,0:T(8,128)(2,1)S(1)} %copy-done.4, bf16[192,4096]{1,0:T(8,128)(2,1)S(1)} %bitcast.23, ...), kind=kOutput, calls=%fused_computation.19 | convolution fusion | flops 1412382720 | bytes 10978048 | tf_op jit(solution)/shard_map/dot_general | solution.py:69
  133.9 0.9 pad_maximum_fusion
  134.8 23.4 %all-to-all-done.4 = bf16[16,192,256]{2,1,0:T(8,128)(2,1)S(1)} async-done(((bf16[16,192,256]{2,1,0:T(8,128)(2,1)}), bf16[16,192,256]{2,1,0:T(8,128)(2,1)S(1)}, u32[]{:S(2)}, u32[]{:S(2)}) %all-to-all-start.4) | async-done | bytes 1572896 | tf_op jit(solution)/shard_map/all_to_all | solution.py:51
  158.2 0.0 all-gather.8.cloned.1.call-update
  158.3 66.9 %all-gather.8.cloned.1.call-done = bf16[3072,1792]{1,0:T(8,128)(2,1)} async-done(((bf16[192,1792]{1,0:T(8,128)(2,1)}), bf16[3072,1792]{1,0:T(8,128)(2,1)}) %all-gather.8.cloned.1.call-update) | async-done | bytes 11010064 | tf_op jit(solution)/shard_map/all_gather | solution.py:79
  225.1 7.2 %convolution_convert_fusion = bf16[256,1792]{1,0:T(8,128)(2,1)S(1)} fusion(bf16[3072,256]{1,0:T(8,128)(2,1)S(1)} %bitcast.19, bf16[3072,1792]{1,0:T(8,128)(2,1)} %all-gather.8.cloned.1.call-done), kind=kOutput, calls=%fused_computation.8 | convolution fusion | flops 2819031040 | bytes 13500416 | tf_op jit(solution)/shard_map/dot_general | solution.py:80
  232.3 1.0 fusion.25
  (9 shorter events, 0.1 us)
Async XLA Ops:
  7.2 2.8 %copy-start = (bf16[256,256]{1,0:T(8,128)(2,1)S(1)}, bf16[256,256]{1,0:T(8,128)(2,1)}, u32[]{:S(2)}) copy-start(bf16[256,256]{1,0:T(8,128)(2,1)} %param.9) | copy-start | bytes 393220
  7.2 74.0 %all-gather.4.cloned.1.call-start = ((), (), s32[]{:S(2)}) async-start(), calls=%async_computation.5 | async-start | bytes 10027008 | tf_op jit(solution)/shard_map/all_gather | solution.py:28
  9.2 118.8 %all-gather.6.cloned.1.call-start = ((), (), s32[]{:S(2)}) async-start(), calls=%async_computation.6 | async-start | bytes 7798784 | tf_op jit(solution)/shard_map/all_gather | solution.py:30
  11.6 7.7 %copy-start.1 = (s32[16,192]{1,0:T(8,128)S(1)}, s32[16,192]{1,0:T(8,128)}, u32[]{:S(2)}) copy-start(s32[16,192]{1,0:T(8,128)} %param.13) | copy-start | bytes 36868
  11.6 7.7 %copy-start.2 = (s32[16]{0:T(128)S(1)}, s32[16]{0:T(128)}, u32[]{:S(2)}) copy-start(s32[16]{0:T(128)} %param.14) | copy-start | bytes 196
  11.6 38.7 %all-to-all-start = ((bf16[16,256,256]{1,2,0:T(8,128)(2,1)}), bf16[16,256,256]{1,2,0:T(8,128)(2,1)S(1)}, u32[]{:S(2)}, u32[]{:S(2)}) async-start(bf16[16,256,256]{1,2,0:T(8,128)(2,1)} %broadcast_in_dim.6), calls=%async_computation | async-start | bytes 4194304 | tf_op jit(solution)/shard_map/all_to_all | solution.py:9
  50.3 3.7 %copy-start.3 = (bf16[4096,512]{1,0:T(8,128)(2,1)S(1)}, bf16[4096,512]{1,0:T(8,128)(2,1)}, u32[]{:S(2)}) copy-start(bf16[4096,512]{1,0:T(8,128)(2,1)} %param.11) | copy-start | bytes 12582916
  50.3 3.7 %copy-start.5 = (f32[512]{0:T(512)S(1)}, f32[512]{0:T(512)}, u32[]{:S(2)}) copy-start(f32[512]{0:T(512)} %param.12) | copy-start | bytes 6148
  56.0 10.3 %all-to-all-start.1 = ((f32[16,1,256]{2,1,0:T(1,128)}), f32[16,1,256]{2,1,0:T(1,128)S(1)}, u32[]{:S(2)}, u32[]{:S(2)}) async-start(f32[16,1,256]{2,1,0:T(1,128)} %broadcast_in_dim.7), calls=%async_computation.1 | async-start | bytes 32768 | tf_op jit(solution)/shard_map/all_to_all | solution.py:9
  70.1 18.3 %all-to-all-start.2 = ((bf16[16,1,192]{2,1,0:T(2,128)(2,1)}), bf16[16,1,192]{2,1,0:T(2,128)(2,1)S(1)}, u32[]{:S(2)}, u32[]{:S(2)}) async-start(bf16[16,1,192]{2,1,0:T(2,128)(2,1)} %all_to_all.24), calls=%async_computation.2 | async-start | bytes 32768 | tf_op jit(solution)/shard_map/all_to_all | solution.py:66
  114.2 44.0 %all-to-all-start.4 = ((bf16[16,192,256]{2,1,0:T(8,128)(2,1)}), bf16[16,192,256]{2,1,0:T(8,128)(2,1)S(1)}, u32[]{:S(2)}, u32[]{:S(2)}) async-start(bf16[16,192,256]{2,1,0:T(8,128)(2,1)} %all_to_all.30), calls=%async_computation.4 | async-start | bytes 3145728 | tf_op jit(solution)/shard_map/all_to_all | solution.py:51
  119.3 105.9 %all-gather.8.cloned.1.call-start = ((), (), s32[]{:S(2)}) async-start(), calls=%async_computation.7 | async-start | bytes 11698176 | tf_op jit(solution)/shard_map/all_gather | solution.py:79
  121.0 7.0 %copy-start.4 = (bf16[192,896]{1,0:T(8,128)(2,1)S(1)}, bf16[192,896]{1,0:T(8,128)(2,1)}, u32[]{:S(2)}) copy-start(bf16[192,896]{1,0:T(8,128)(2,1)} %param.17) | copy-start | bytes 1032196
Sparse Core Ops, SparseCore 0:
  9.8 64.9 all-gather.3
  76.7 51.3 all-gather.5
  158.4 66.7 all-gather.7
where the time goes:
time: 240 us
  waiting for transfers between devices  134 us (56%)
  matrix products  28.9 us (12%)
  starting transfers between devices  27.7 us (12%)
  blocking collectives  25.6 us (11%)
  between operations  13.9 us (6%)
  local copies, waits for them, and re-layouts  5.97 us (2%)
  other arithmetic  3.59 us (1%)
    all_gather x1, waiting for transfers between devices, on_device(): both_d = lax.all_gather(d_both, 'dp', axis=0, tiled=True)  66.9 us
    all_to_all x2, waiting for transfers between devices, gather_by_a2a(): lax.all_to_all(jnp.broadcast_to(x[None], (parts,) + x.shape), axis_name,...  37.1 us
    all_to_all x1, blocking collectives, gather_by_a2a(): lax.all_to_all(jnp.broadcast_to(x[None], (parts,) + x.shape), axis_name,...  25.6 us
    all_to_all x1, waiting for transfers between devices, on_device(): lax.all_to_all(row_blocks, 'dp', split_axis=0, concat_axis=0, tiled=True)  23.4 us
    all_to_all x2, starting transfers between devices, gather_by_a2a(): lax.all_to_all(jnp.broadcast_to(x[None], (parts,) + x.shape), axis_name,...  11.6 us
    all_to_all x1, starting transfers between devices, on_device(): lax.all_to_all(picked_weight, 'dp', split_axis=0, concat_axis=0, tiled=True)  11 us
    dot_general x1, matrix products, on_device(): lax.dot_general(row_slices, both_d, contract_rows, preferred_element_type...  7.17 us
    dot_general x1, matrix products, on_device(): up = jnp.dot(row_x, full_w[1], preferred_element_type=jnp.float32)  5.92 us
  transfers between devices with their start and end apart: 7, of which 6 were waited for; matrix products, arithmetic and copies ran while one was open for 12% of the time, Pallas kernels for 0%

commit v1 on v0

--- a/solution.py
+++ b/solution.py
@@ -76,7 +76,8 @@
     d_both, row_slices = lax.optimization_barrier(
         (jnp.concatenate([d_gate, d_up], axis=1), row_slices)
     )
-    both_d = lax.all_gather(d_both, "dp", axis=0, tiled=True)
+    outgoing = jnp.stack([d_both] * lax.axis_size("dp"))
+    both_d = jnp.concatenate(lax.all_to_all(outgoing, "dp", 0, 0), axis=0)
     grads = lax.dot_general(
         row_slices, both_d, contract_rows, preferred_element_type=jnp.float32
     ).astype(jnp.bfloat16)

time: 240 us -> 421 us (1.75)
  blocking collectives: 25.6 us -> 272 us
  waiting for transfers between devices: 134 us -> 68.1 us
  local copies, waits for them, and re-layouts: 5.97 us -> 11.2 us
    all_to_all x0 -> x1, blocking collectives: none -> 246 us  [on_device(): both_d = jnp.concatenate(lax.all_to_all(outgoing, 'dp', 0, 0), axis=0)]
    all_gather x1 -> x0, waiting for transfers between devices: 66.9 us -> none  [on_device(): both_d = lax.all_gather(d_both, 'dp', axis=0, tiled=True)]
    another operation x0 -> x1, local copies, waits for them, and re-layouts: none -> 5.25 us  [on_device(): outgoing = jnp.stack([d_both] * lax.axis_size('dp'))]
  transfers between devices with their start and end apart: 7 -> 6, of which waited for: 6 -> 5; matrix products, arithmetic and copies ran while one was open for 12% -> 6% of each run, Pallas kernels for 0% -> 0%
where the time goes in v1:
time: 421 us
  blocking collectives  272 us (65%)
  waiting for transfers between devices  68.1 us (16%)
  starting transfers between devices  27.7 us (7%)
  matrix products  24.8 us (6%)
  between operations  14.2 us (3%)
  local copies, waits for them, and re-layouts  11.2 us (3%)
    all_to_all x1, blocking collectives, on_device(): both_d = jnp.concatenate(lax.all_to_all(outgoing, 'dp', 0, 0), axis=0)  246 us
    all_to_all x2, waiting for transfers between devices, gather_by_a2a(): lax.all_to_all(jnp.broadcast_to(x[None], (parts,) + x.shape), axis_name,...  37.1 us
    all_to_all x1, blocking collectives, gather_by_a2a(): lax.all_to_all(jnp.broadcast_to(x[None], (parts,) + x.shape), axis_name,...  25.6 us
    all_to_all x1, waiting for transfers between devices, on_device(): lax.all_to_all(row_blocks, 'dp', split_axis=0, concat_axis=0, tiled=True)  24.2 us
    all_to_all x2, starting transfers between devices, gather_by_a2a(): lax.all_to_all(jnp.broadcast_to(x[None], (parts,) + x.shape), axis_name,...  11.6 us
    all_to_all x1, starting transfers between devices, on_device(): lax.all_to_all(picked_weight, 'dp', split_axis=0, concat_axis=0, tiled=True)  11 us
  transfers between devices with their start and end apart: 6, of which 5 were waited for; matrix products, arithmetic and copies ran while one was open for 6% of the time, Pallas kernels for 0%

profile of v1, /device:TPU:1, one launch (start us, length us, event | category | flops | bytes accessed | tf_op | source)
XLA Modules:
  0.0 420.8 jit_solution(3784547371898635857)
XLA Ops:
  7.2 0.0 copy-start
  7.2 0.0 all-gather.3.cloned.1.call-start
  7.2 2.0 pad_maximum_fusion.1
  9.2 0.0 all-gather.3.cloned.1.call-update
  9.2 0.0 all-gather.5.cloned.1.call-start
  9.3 0.7 all-gather.5.cloned.1.call-update
  10.0 0.0 copy-done
  10.0 0.1 copy.22
  10.1 1.5 broadcast_in_dim.6
  11.6 0.0 copy-start.1
  11.6 0.0 copy-start.2
  11.6 7.7 %all-to-all-start = ((bf16[16,256,256]{1,2,0:T(8,128)(2,1)}), bf16[16,256,256]{1,2,0:T(8,128)(2,1)S(1)}, u32[]{:S(2)}, u32[]{:S(2)}) async-start(bf16[16,256,256]{1,2,0:T(8,128)(2,1)} %broadcast_in_dim.6), calls=%async_computation | async-start | bytes 4194304 | tf_op jit(solution)/shard_map/all_to_all | solution.py:9
  19.3 0.0 copy-done.1
  19.3 0.0 copy-done.2
  19.3 0.1 fusion.22
  19.4 30.8 %all-to-all-done = bf16[16,256,256]{1,2,0:T(8,128)(2,1)S(1)} async-done(((bf16[16,256,256]{1,2,0:T(8,128)(2,1)}), bf16[16,256,256]{1,2,0:T(8,128)(2,1)S(1)}, u32[]{:S(2)}, u32[]{:S(2)}) %all-to-all-start) | async-done | bytes 2097184 | tf_op jit(solution)/shard_map/all_to_all | solution.py:9
  50.3 0.0 copy-start.5
  50.3 3.7 fusion.26
  54.0 0.0 copy-done.3
  54.0 0.0 copy-done.5
  54.0 1.4 fusion.14
  55.4 0.6 broadcast_in_dim.7
  56.0 3.9 all-to-all-start.1
  59.9 0.1 and.37
  60.0 0.1 eq.38
  60.1 6.2 %all-to-all-done.1 = f32[16,1,256]{2,1,0:T(1,128)S(1)} async-done(((f32[16,1,256]{2,1,0:T(1,128)}), f32[16,1,256]{2,1,0:T(1,128)S(1)}, u32[]{:S(2)}, u32[]{:S(2)}) %all-to-all-start.1) | async-done | bytes 16416 | tf_op jit(solution)/shard_map/all_to_all | solution.py:9
  66.4 0.6 fusion.24
  66.9 2.5 fusion.6
  69.4 0.7 all_to_all.28
  70.1 11.0 %all-to-all-start.2 = ((bf16[16,1,192]{2,1,0:T(2,128)(2,1)}), bf16[16,1,192]{2,1,0:T(2,128)(2,1)S(1)}, u32[]{:S(2)}, u32[]{:S(2)}) async-start(bf16[16,1,192]{2,1,0:T(2,128)(2,1)} %all_to_all.28), calls=%async_computation.2 | async-start | bytes 32768 | tf_op jit(solution)/shard_map/all_to_all | solution.py:66
  81.2 0.0 all-gather.3.cloned.1.call-done
  81.2 2.4 fusion.15
  83.5 4.9 %all-to-all-done.2 = bf16[16,1,192]{2,1,0:T(2,128)(2,1)S(1)} async-done(((bf16[16,1,192]{2,1,0:T(2,128)(2,1)}), bf16[16,1,192]{2,1,0:T(2,128)(2,1)S(1)}, u32[]{:S(2)}, u32[]{:S(2)}) %all-to-all-start.2) | async-done | bytes 6176 | tf_op jit(solution)/shard_map/all_to_all | solution.py:66
  88.5 0.1 broadcast_in_dim.8
  88.6 25.6 %all_to_all.35 = bf16[16,192,256]{2,1,0:T(8,128)(2,1)} all-to-all(bf16[16,192,256]{2,1,0:T(8,128)(2,1)S(1)} %broadcast_in_dim.8), channel_id=1, replica_groups=mesh['dp'=16,'mp'=16] {'mp'}, dimensions={0} | all-to-all | bytes 3145728 | tf_op jit(solution)/shard_map/all_to_all | solution.py:9
  114.2 5.0 %all-to-all-start.4 = ((bf16[16,192,256]{2,1,0:T(8,128)(2,1)}), bf16[16,192,256]{2,1,0:T(8,128)(2,1)S(1)}, u32[]{:S(2)}, u32[]{:S(2)}) async-start(bf16[16,192,256]{2,1,0:T(8,128)(2,1)} %all_to_all.35), calls=%async_computation.4 | async-start | bytes 3145728 | tf_op jit(solution)/shard_map/all_to_all | solution.py:51
  119.3 1.6 copy.27
  120.9 0.0 copy-start.4
  121.0 5.9 %fusion = f32[192,896]{1,0:T(8,128)} fusion(bf16[192,4096]{1,0:T(8,128)(2,1)S(1)} %bitcast.24, bf16[4096,1152]{1,0:T(8,128)(2,1)} %all-gather.3.cloned.1.call-done), kind=kOutput, calls=%fused_computation | convolution fusion | flops 1409286144 | bytes 9601024 | tf_op jit(solution)/shard_map/dot_general | solution.py:68
  126.9 1.2 all-gather.5.cloned.1.call-done
  128.0 0.0 copy-done.4
  128.0 5.9 %multiply_convert_fusion = (bf16[192,896]{1,0:T(8,128)(2,1)}, bf16[192,896]{1,0:T(8,128)(2,1)S(1)}, bf16[192,896]{1,0:T(8,128)(2,1)S(1)}) fusion(f32[192,896]{1,0:T(8,128)} %fusion, f32[192]{0:T(256)S(1)} %convert_reduce_fusion, bf16[192,896]{1,0:T(8,128)(2,1)S(1)} %copy-done.4, bf16[192,4096]{1,0:T(8,128)(2,1)S(1)} %bitcast.25, ...), kind=kOutput, calls=%fused_computation.19 | convolution fusion | flops 1412382720 | bytes 10978048 | tf_op jit(solution)/shard_map/dot_general | solution.py:69
  133.9 0.1 pad_maximum_fusion
  134.0 24.2 %all-to-all-done.4 = bf16[16,192,256]{2,1,0:T(8,128)(2,1)S(1)} async-done(((bf16[16,192,256]{2,1,0:T(8,128)(2,1)}), bf16[16,192,256]{2,1,0:T(8,128)(2,1)S(1)}, u32[]{:S(2)}, u32[]{:S(2)}) %all-to-all-start.4) | async-done | bytes 1572896 | tf_op jit(solution)/shard_map/all_to_all | solution.py:51
  158.2 5.3 %stack.2 = bf16[16,192,1792]{2,1,0:T(8,128)(2,1)} broadcast(bf16[192,1792]{1,0:T(8,128)(2,1)S(1)} %pad_maximum_fusion), dimensions={1,2} | broadcast | bytes 11698176 | tf_op jit(solution)/shard_map/stack | solution.py:79
  163.5 246.4 %all_to_all.36 = bf16[16,192,1792]{2,1,0:T(8,128)(2,1)S(1)} all-to-all(bf16[16,192,1792]{2,1,0:T(8,128)(2,1)} %stack.2), channel_id=1, replica_groups=mesh['dp'=16,'mp'=16] {'dp'}, dimensions={0} | all-to-all | bytes 22020096 | tf_op jit(solution)/shard_map/all_to_all | solution.py:80
  409.9 3.0 convolution_convert_fusion
  413.0 1.0 fusion.25
  (8 shorter events, 0.1 us)
Async XLA Ops:
  7.2 2.8 copy-start
  7.2 74.0 %all-gather.3.cloned.1.call-start = ((), (), s32[]{:S(2)}) async-start(), calls=%async_computation.6 | async-start | bytes 10027008 | tf_op jit(solution)/shard_map/all_gather | solution.py:28
  9.2 118.8 %all-gather.5.cloned.1.call-start = ((), (), s32[]{:S(2)}) async-start(), calls=%async_computation.7 | async-start | bytes 7798784 | tf_op jit(solution)/shard_map/all_gather | solution.py:30
  11.6 7.7 %copy-start.1 = (s32[16,192]{1,0:T(8,128)S(1)}, s32[16,192]{1,0:T(8,128)}, u32[]{:S(2)}) copy-start(s32[16,192]{1,0:T(8,128)} %param.13) | copy-start | bytes 36868
  11.6 7.7 %copy-start.2 = (s32[16]{0:T(128)S(1)}, s32[16]{0:T(128)}, u32[]{:S(2)}) copy-start(s32[16]{0:T(128)} %param.14) | copy-start | bytes 196
  11.6 38.7 %all-to-all-start = ((bf16[16,256,256]{1,2,0:T(8,128)(2,1)}), bf16[16,256,256]{1,2,0:T(8,128)(2,1)S(1)}, u32[]{:S(2)}, u32[]{:S(2)}) async-start(bf16[16,256,256]{1,2,0:T(8,128)(2,1)} %broadcast_in_dim.6), calls=%async_computation | async-start | bytes 4194304 | tf_op jit(solution)/shard_map/all_to_all | solution.py:9
  50.3 3.7 copy-start.3
  50.3 3.7 copy-start.5
  56.0 10.3 %all-to-all-start.1 = ((f32[16,1,256]{2,1,0:T(1,128)}), f32[16,1,256]{2,1,0:T(1,128)S(1)}, u32[]{:S(2)}, u32[]{:S(2)}) async-start(f32[16,1,256]{2,1,0:T(1,128)} %broadcast_in_dim.7), calls=%async_computation.1 | async-start | bytes 32768 | tf_op jit(solution)/shard_map/all_to_all | solution.py:9
  70.1 18.3 %all-to-all-start.2 = ((bf16[16,1,192]{2,1,0:T(2,128)(2,1)}), bf16[16,1,192]{2,1,0:T(2,128)(2,1)S(1)}, u32[]{:S(2)}, u32[]{:S(2)}) async-start(bf16[16,1,192]{2,1,0:T(2,128)(2,1)} %all_to_all.28), calls=%async_computation.2 | async-start | bytes 32768 | tf_op jit(solution)/shard_map/all_to_all | solution.py:66
  114.2 44.0 %all-to-all-start.4 = ((bf16[16,192,256]{2,1,0:T(8,128)(2,1)}), bf16[16,192,256]{2,1,0:T(8,128)(2,1)S(1)}, u32[]{:S(2)}, u32[]{:S(2)}) async-start(bf16[16,192,256]{2,1,0:T(8,128)(2,1)} %all_to_all.35), calls=%async_computation.4 | async-start | bytes 3145728 | tf_op jit(solution)/shard_map/all_to_all | solution.py:51
  120.9 7.1 %copy-start.4 = (bf16[192,896]{1,0:T(8,128)(2,1)S(1)}, bf16[192,896]{1,0:T(8,128)(2,1)}, u32[]{:S(2)}) copy-start(bf16[192,896]{1,0:T(8,128)(2,1)} %param.17) | copy-start | bytes 1032196
Sparse Core Ops, SparseCore 0:
  9.8 64.9 all-gather.2
  76.7 51.3 all-gather.4
